TPU v7x, 256 devices: a whole 4x4x8 slice. The times are simulated.
256 devices in a mesh: src: 8 (over y, core), tgt: 32 (over z, x).
Axes of the slice: x: 4, y: 4, z: 8, core: 2. Of those that a mesh axis runs over, the one named last changes fastest.
Arguments:
- src_embed: bfloat16 [8192, 256], P('src'), may hold values from -128 to 128
- tgt_embed: bfloat16 [155648, 256], P('tgt'), may hold values from -1 to 1
- qwen_embed: bfloat16 [155648, 256], P('tgt'), may hold values from -6 to 6
- other_log: float32 [155648], P('tgt'), may hold values from -12 to -10
- src_counts: int32 [8192], P('src'), may hold values from 1 to 999
- tgt_counts: int32 [155648], P('tgt'), may hold values from 1 to 999
Outputs:
- transported: float32 [8192, 256], P(('src', 'tgt'))
All inputs are finite; a program needn't handle non-finite values.
Results may differ from a plain program's by a relative error of at most 0.0034.
Values sent between devices are 32-bit elements; how exact they have to be, the bound alone decides.
A program may use at most 128 MiB of HBM per device.

v0:
```python
import jax
import jax.numpy as jnp
from jax import lax
from jax.sharding import PartitionSpec as P

ITERS = 2
inv_temp = 4.0


def logits_of(src_embed, tgt_embed):
    products = lax.dot_general(
        src_embed, tgt_embed, (((1,), (1,)), ((), ())), preferred_element_type=jnp.float32
    )
    return products * inv_temp


def row_lse(values):
    local_peak = jnp.max(values, axis=1)
    peak = lax.pmax(local_peak, "tgt")
    total = lax.psum(jnp.sum(jnp.exp(values - peak[:, None]), axis=1), "tgt")
    return peak + jnp.log(total)


def col_lse(values):
    local_peak = jnp.max(values, axis=0)
    peak = lax.pmax(local_peak, "src")
    total = lax.psum(jnp.sum(jnp.exp(values - peak[None, :]), axis=0), "src")
    return peak + jnp.log(total)


def on_device(src_embed, tgt_embed, qwen_embed, other_log, src_counts, tgt_counts):
    src_float = src_counts.astype(jnp.float32)
    tgt_float = tgt_counts.astype(jnp.float32)
    slab_sum = lax.psum(jnp.sum(src_float), "src")
    vocab_sum = lax.psum(jnp.sum(tgt_float), "tgt")
    src_log = jnp.log(src_float) - jnp.log(slab_sum)
    tgt_log = jnp.log(tgt_float) - jnp.log(vocab_sum)
    stored = logits_of(src_embed, tgt_embed)

    def current():
        return stored

    col_pot = jnp.zeros((tgt_embed.shape[0],), jnp.float32)
    row_pot = jnp.zeros((src_embed.shape[0],), jnp.float32)
    for sweep in range(ITERS):
        row_pot = src_log - row_lse(current() + col_pot[None, :])
        col_pot = tgt_log - jnp.logaddexp(col_lse(current() + row_pot[:, None]), other_log)
    shift = row_pot - src_log
    weights = jnp.exp(shift[:, None] + col_pot[None, :] + current()).astype(jnp.bfloat16)
    owned_rows = src_embed.shape[0] // lax.axis_size("tgt")
    partial_rows = jnp.dot(weights, qwen_embed, preferred_element_type=jnp.float32)
    summed = lax.psum(partial_rows, "tgt")
    return lax.dynamic_slice_in_dim(summed, lax.axis_index("tgt") * owned_rows, owned_rows, 0)


def solution(mesh):
    return jax.shard_map(
        on_device,
        mesh=mesh,
        in_specs=(P("src", None), P("tgt", None), P("tgt", None), P("tgt"), P("src"), P("tgt")),
        out_specs=P(("src", "tgt"), None),
        check_vma=False,
    )
```

profile of v0, /device:TPU:8, one launch (start us, length us, event | category | flops | bytes accessed | tf_op | source)
XLA Modules:
  0.0 646.8 jit_solution(11345955397474943461)
XLA Ops:
  6.5 0.0 copy-start
  6.5 0.0 all-reduce.3.cloned.1.call-start
  6.5 1.5 convert_reduce_fusion
  8.0 1.3 convert_reduce_fusion.1
  9.3 0.0 copy-done
  9.3 0.0 copy-start.3
  9.3 9.3 %fusion.4 = (f32[1024]{0:T(1024)S(1)}, f32[1024,4864]{1,0:T(8,128)}) fusion(bf16[1024,256]{1,0:T(8,128)(2,1)} %param.6, bf16[4864,256]{1,0:T(8,128)(2,1)S(1)} %copy-done), kind=kOutput, calls=%fused_computation.24 | convolution fusion | flops 2560097280 | bytes 22941696 | tf_op jit(solution)/shard_map/dot_general | solution.py:11
  18.7 77.7 %pmax.28 = f32[1024]{0:T(1024)S(1)} all-reduce(f32[1024]{0:T(1024)S(1)} %get-tuple-element.9), channel_id=1, replica_groups=mesh['src'=8,'tgt'=32] {'tgt'}, use_global_device_ids=true, to_apply=%region_5.0 | all-reduce | flops 1024 | bytes 8192 | tf_op jit(solution)/shard_map/pmax | solution.py:19
  96.3 10.6 %psum.49 = f32[]{:T(128)} all-reduce(f32[]{:T(128)} %convert_reduce_fusion.1), channel_id=1, replica_groups=mesh['src'=8,'tgt'=32] {'src'}, use_global_device_ids=true, to_apply=%region_1.0 | all-reduce | flops 1 | bytes 8 | tf_op jit(solution)/shard_map/psum | solution.py:34
  107.7 9.4 %exponential_reduce_fusion.3 = f32[1024]{0:T(1024)S(1)} fusion(f32[1024,4864]{1,0:T(8,128)} %get-tuple-element.10, f32[1024]{0:T(1024)S(1)} %pmax.28), kind=kLoop, calls=%fused_computation.4 | loop fusion | flops 9960448 | bytes 19931136 | tf_op jit(solution)/shard_map/reduce_sum | solution.py:20
  117.1 71.1 %all-reduce = (f32[1024]{0:T(1024)S(1)}, f32[]{:T(128)}) all-reduce(f32[1024]{0:T(1024)S(1)} %exponential_reduce_fusion.3, f32[]{:T(128)} %convert_reduce_fusion), channel_id=1, replica_groups=mesh['src'=8,'tgt'=32] {'tgt'}, use_global_device_ids=true, to_apply=%region_7.0 | all-reduce | flops 1025 | bytes 8200 | tf_op jit(solution)/shard_map/psum | solution.py:20
  188.2 0.0 copy-done.3
  188.2 0.0 copy-start.1
  188.2 0.0 copy-start.2
  188.2 8.3 %add_reduce_fusion.2 = f32[4864]{0:T(1024)S(1)} fusion(f32[1024,4864]{1,0:T(8,128)} %get-tuple-element.10, f32[1024]{0:T(1024)S(1)} %add_subtract_fusion.1), kind=kLoop, calls=%fused_computation.7 | loop fusion | flops 9956608 | bytes 19946496 | tf_op jit(solution)/shard_map/reduce_max | solution.py:25
  196.5 23.0 %pmax.29 = f32[4864]{0:T(1024)S(1)} all-reduce(f32[4864]{0:T(1024)S(1)} %add_reduce_fusion.2), channel_id=1, replica_groups=mesh['src'=8,'tgt'=32] {'src'}, use_global_device_ids=true, to_apply=%region_9.0 | all-reduce | flops 4864 | bytes 38912 | tf_op jit(solution)/shard_map/pmax | solution.py:26
  219.5 10.9 %exponential_reduce_fusion.2 = f32[4864]{0:T(1024)S(1)} fusion(f32[1024,4864]{1,0:T(8,128)} %get-tuple-element.10, f32[4864]{0:T(1024)S(1)} %pmax.29, f32[1024]{0:T(1024)S(1)} %add_subtract_fusion.1), kind=kLoop, calls=%fused_computation.3 | loop fusion | flops 14937344 | bytes 19965952 | tf_op jit(solution)/shard_map/reduce_sum | solution.py:27
  230.4 23.8 %psum.52 = f32[4864]{0:T(1024)S(1)} all-reduce(f32[4864]{0:T(1024)S(1)} %exponential_reduce_fusion.2), channel_id=1, replica_groups=mesh['src'=8,'tgt'=32] {'src'}, use_global_device_ids=true, to_apply=%region_11.0 | all-reduce | flops 4864 | bytes 38912 | tf_op jit(solution)/shard_map/psum | solution.py:27
  254.9 0.0 copy-done.1
  254.9 0.0 copy-done.2
  254.9 8.1 %add_reduce_fusion.1 = f32[1024]{0:T(1024)S(1)} fusion(f32[1024,4864]{1,0:T(8,128)} %get-tuple-element.10, f32[4864]{0:T(1024)S(1)} %select_subtract_fusion.1), kind=kLoop, calls=%fused_computation.6 | loop fusion | flops 9960448 | bytes 19946496 | tf_op jit(solution)/shard_map/reduce_max | solution.py:18
  263.0 71.6 %pmax.30 = f32[1024]{0:T(1024)S(1)} all-reduce(f32[1024]{0:T(1024)S(1)} %add_reduce_fusion.1), channel_id=1, replica_groups=mesh['src'=8,'tgt'=32] {'tgt'}, use_global_device_ids=true, to_apply=%region_13.0 | all-reduce | flops 1024 | bytes 8192 | tf_op jit(solution)/shard_map/pmax | solution.py:19
  334.6 10.0 %exponential_reduce_fusion.1 = f32[1024]{0:T(1024)S(1)} fusion(f32[1024,4864]{1,0:T(8,128)} %get-tuple-element.10, f32[1024]{0:T(1024)S(1)} %pmax.30, f32[4864]{0:T(1024)S(1)} %select_subtract_fusion.1), kind=kLoop, calls=%fused_computation.2 | loop fusion | flops 14941184 | bytes 19950592 | tf_op jit(solution)/shard_map/reduce_sum | solution.py:20
  344.7 69.6 %psum.53 = f32[1024]{0:T(1024)S(1)} all-reduce(f32[1024]{0:T(1024)S(1)} %exponential_reduce_fusion.1), channel_id=1, replica_groups=mesh['src'=8,'tgt'=32] {'tgt'}, use_global_device_ids=true, to_apply=%region_15.0 | all-reduce | flops 1024 | bytes 8192 | tf_op jit(solution)/shard_map/psum | solution.py:20
  414.3 8.3 %add_reduce_fusion = f32[4864]{0:T(1024)S(1)} fusion(f32[1024,4864]{1,0:T(8,128)} %get-tuple-element.10, f32[1024]{0:T(1024)S(1)} %get-tuple-element.8), kind=kLoop, calls=%fused_computation.5 | loop fusion | flops 9956608 | bytes 19946496 | tf_op jit(solution)/shard_map/reduce_max | solution.py:25
  422.6 23.6 %pmax.31 = f32[4864]{0:T(1024)S(1)} all-reduce(f32[4864]{0:T(1024)S(1)} %add_reduce_fusion), channel_id=1, replica_groups=mesh['src'=8,'tgt'=32] {'src'}, use_global_device_ids=true, to_apply=%region_17.0 | all-reduce | flops 4864 | bytes 38912 | tf_op jit(solution)/shard_map/pmax | solution.py:26
  446.2 10.9 %exponential_reduce_fusion = f32[4864]{0:T(1024)S(1)} fusion(f32[1024,4864]{1,0:T(8,128)} %get-tuple-element.10, f32[4864]{0:T(1024)S(1)} %pmax.31, f32[1024]{0:T(1024)S(1)} %get-tuple-element.8), kind=kLoop, calls=%fused_computation.1 | loop fusion | flops 14937344 | bytes 19965952 | tf_op jit(solution)/shard_map/reduce_sum | solution.py:27
  457.1 23.8 %psum.54 = f32[4864]{0:T(1024)S(1)} all-reduce(f32[4864]{0:T(1024)S(1)} %exponential_reduce_fusion), channel_id=1, replica_groups=mesh['src'=8,'tgt'=32] {'src'}, use_global_device_ids=true, to_apply=%region_19.0 | all-reduce | flops 4864 | bytes 38912 | tf_op jit(solution)/shard_map/psum | solution.py:27
  480.9 11.5 %fusion = f32[1024,256]{1,0:T(8,128)} fusion(bf16[4864,256]{1,0:T(8,128)(2,1)} %param.8, f32[1024,4864]{1,0:T(8,128)} %get-tuple-element.10, f32[4864]{0:T(1024)S(1)} %select_subtract_fusion, f32[1024]{0:T(1024)S(1)} %get-tuple-element.7), kind=kOutput, calls=%fused_computation.9 | convolution fusion | flops 2565079040 | bytes 23485440 | tf_op jit(solution)/shard_map/dot_general | solution.py:51
  492.4 0.0 all-reduce.3.cloned.1.call-update
  492.5 146.1 %all-reduce.3.cloned.1.call-done = f32[1024,256]{1,0:T(8,128)} async-done(((f32[1024,256]{1,0:T(8,128)}), f32[1024,256]{1,0:T(8,128)}) %all-reduce.3.cloned.1.call-update) | async-done | bytes 1048592 | tf_op jit(solution)/shard_map/psum | solution.py:52
  638.6 1.4 constant_dynamic-slice_fusion
  (4 shorter events, 0.1 us)
Async XLA Ops:
  6.5 2.8 copy-start
  6.5 632.0 %all-reduce.3.cloned.1.call-start = ((), (), s32[]{:S(2)}) async-start(), calls=%async_computation | async-start | bytes 2097152 | tf_op jit(solution)/shard_map/psum | solution.py:52
  9.3 178.9 %copy-start.3 = (s32[1024]{0:T(1024)S(1)}, s32[1024]{0:T(1024)}, u32[]{:S(2)}) copy-start(s32[1024]{0:T(1024)} %param.10) | copy-start | bytes 12292
  188.2 66.7 %copy-start.1 = (s32[4864]{0:T(1024)S(1)}, s32[4864]{0:T(1024)}, u32[]{:S(2)}) copy-start(s32[4864]{0:T(1024)} %param.11) | copy-start | bytes 58372
  188.2 66.7 %copy-start.2 = (f32[4864]{0:T(1024)S(1)}, f32[4864]{0:T(1024)}, u32[]{:S(2)}) copy-start(f32[4864]{0:T(1024)} %param.9) | copy-start | bytes 58372
Sparse Core Ops, SparseCore 0:
  492.6 145.9 all-reduce.2
where the time goes:
time: 647 us
  blocking collectives  395 us (61%)
  waiting for transfers between devices  146 us (23%)
  other arithmetic  68.7 us (11%)
  matrix products  20.8 us (3%)
  between operations  14.8 us (2%)
    pmax x2, blocking collectives, row_lse(): peak = lax.pmax(local_peak, 'tgt')  149 us
    psum x1, waiting for transfers between devices, on_device(): summed = lax.psum(partial_rows, 'tgt')  146 us
    psum x2, blocking collectives, row_lse(): total = lax.psum(jnp.sum(jnp.exp(values - peak[:, None]), axis=1), 'tgt')  141 us
    psum x2, blocking collectives, col_lse(): total = lax.psum(jnp.sum(jnp.exp(values - peak[None, :]), axis=0), 'src')  47.6 us
    pmax x2, blocking collectives, col_lse(): peak = lax.pmax(local_peak, 'src')  46.6 us
    reduce_sum x2, other arithmetic, col_lse(): total = lax.psum(jnp.sum(jnp.exp(values - peak[None, :]), axis=0), 'src')  21.7 us
    reduce_sum x2, other arithmetic, row_lse(): total = lax.psum(jnp.sum(jnp.exp(values - peak[:, None]), axis=1), 'tgt')  19.4 us
    reduce_max x2, other arithmetic, col_lse(): local_peak = jnp.max(values, axis=0)  16.6 us
  transfers between devices with their start and end apart: 1, of which 1 were waited for; matrix products, arithmetic and copies ran while one was open for 0% of the time, Pallas kernels for 0%

commit v1 on v0

--- a/solution.py
+++ b/solution.py
@@ -49,7 +49,9 @@
     weights = jnp.exp(shift[:, None] + col_pot[None, :] + current()).astype(jnp.bfloat16)
     owned_rows = src_embed.shape[0] // lax.axis_size("tgt")
     partial_rows = jnp.dot(weights, qwen_embed, preferred_element_type=jnp.float32)
-    summed = lax.psum(partial_rows, "tgt")
+    summed = partial_rows
+    for hop in (1, 2, 4, 8, 16):
+        summed = summed + lax.ppermute(summed, "tgt", [(dev, dev ^ hop) for dev in range(32)])
     return lax.dynamic_slice_in_dim(summed, lax.axis_index("tgt") * owned_rows, owned_rows, 0)
 
 

time: 647 us -> 677 us (1.046)
  the two profiles are of different devices: /device:TPU:8 before, /device:TPU:10 now
where the time goes in v1:
time: 677 us
  blocking collectives  395 us (58%)
  waiting for transfers between devices  190 us (28%)
  other arithmetic  70.6 us (10%)
  matrix products  18.5 us (3%)
    ppermute x5, waiting for transfers between devices, on_device(): lax.ppermute(summed, 'tgt', [(dev, dev ^ hop) for dev in range(32)])  190 us
    psum x2, blocking collectives, row_lse(): total = lax.psum(jnp.sum(jnp.exp(values - peak[:, None]), axis=1), 'tgt')  147 us
    pmax x2, blocking collectives, row_lse(): peak = lax.pmax(local_peak, 'tgt')  143 us
    psum x2, blocking collectives, col_lse(): total = lax.psum(jnp.sum(jnp.exp(values - peak[None, :]), axis=0), 'src')  47.6 us
    pmax x2, blocking collectives, col_lse(): peak = lax.pmax(local_peak, 'src')  46.5 us
    reduce_sum x2, other arithmetic, col_lse(): total = lax.psum(jnp.sum(jnp.exp(values - peak[None, :]), axis=0), 'src')  21.7 us
    reduce_sum x2, other arithmetic, row_lse(): total = lax.psum(jnp.sum(jnp.exp(values - peak[:, None]), axis=1), 'tgt')  19.4 us
    reduce_max x2, other arithmetic, col_lse(): local_peak = jnp.max(values, axis=0)  16.6 us
  transfers between devices with their start and end apart: 5, of which 5 were waited for; matrix products, arithmetic and copies ran while one was open for 0% of the time, Pallas kernels for 0%

profile of v1, /device:TPU:10, one launch (start us, length us, event | category | flops | bytes accessed | tf_op | source)
XLA Modules:
  0.0 676.5 jit_solution(12611341516364978688)
XLA Ops:
  0.0 0.0 copy-start
  0.0 1.5 convert_reduce_fusion
  1.5 1.3 convert_reduce_fusion.1
  2.8 0.0 copy-done
  2.8 0.0 copy-start.3
  2.8 9.3 %fusion.4 = (f32[1024]{0:T(1024)S(1)}, f32[1024,4864]{1,0:T(8,128)}) fusion(bf16[1024,256]{1,0:T(8,128)(2,1)} %param.6, bf16[4864,256]{1,0:T(8,128)(2,1)S(1)} %copy-done), kind=kOutput, calls=%fused_computation.24 | convolution fusion | flops 2560097280 | bytes 22941696 | tf_op jit(solution)/shard_map/dot_general | solution.py:11
  12.1 73.7 %pmax.28 = f32[1024]{0:T(1024)S(1)} all-reduce(f32[1024]{0:T(1024)S(1)} %get-tuple-element.9), channel_id=1, replica_groups=mesh['src'=8,'tgt'=32] {'tgt'}, use_global_device_ids=true, to_apply=%region_5.0 | all-reduce | flops 1024 | bytes 8192 | tf_op jit(solution)/shard_map/pmax | solution.py:19
  85.8 10.6 %psum.42 = f32[]{:T(128)} all-reduce(f32[]{:T(128)} %convert_reduce_fusion.1), channel_id=1, replica_groups=mesh['src'=8,'tgt'=32] {'src'}, use_global_device_ids=true, to_apply=%region_1.0 | all-reduce | flops 1 | bytes 8 | tf_op jit(solution)/shard_map/psum | solution.py:34
  97.1 9.4 %exponential_reduce_fusion.3 = f32[1024]{0:T(1024)S(1)} fusion(f32[1024,4864]{1,0:T(8,128)} %get-tuple-element.10, f32[1024]{0:T(1024)S(1)} %pmax.28), kind=kLoop, calls=%fused_computation.4 | loop fusion | flops 9960448 | bytes 19931136 | tf_op jit(solution)/shard_map/reduce_sum | solution.py:20
  106.5 75.7 %all-reduce = (f32[1024]{0:T(1024)S(1)}, f32[]{:T(128)}) all-reduce(f32[1024]{0:T(1024)S(1)} %exponential_reduce_fusion.3, f32[]{:T(128)} %convert_reduce_fusion), channel_id=1, replica_groups=mesh['src'=8,'tgt'=32] {'tgt'}, use_global_device_ids=true, to_apply=%region_7.0 | all-reduce | flops 1025 | bytes 8200 | tf_op jit(solution)/shard_map/psum | solution.py:20
  182.2 0.0 copy-done.3
  182.2 0.0 copy-start.1
  182.2 0.0 copy-start.2
  182.2 8.3 %add_reduce_fusion.2 = f32[4864]{0:T(1024)S(1)} fusion(f32[1024,4864]{1,0:T(8,128)} %get-tuple-element.10, f32[1024]{0:T(1024)S(1)} %add_subtract_fusion.1), kind=kLoop, calls=%fused_computation.7 | loop fusion | flops 9956608 | bytes 19946496 | tf_op jit(solution)/shard_map/reduce_max | solution.py:25
  190.5 23.0 %pmax.29 = f32[4864]{0:T(1024)S(1)} all-reduce(f32[4864]{0:T(1024)S(1)} %add_reduce_fusion.2), channel_id=1, replica_groups=mesh['src'=8,'tgt'=32] {'src'}, use_global_device_ids=true, to_apply=%region_9.0 | all-reduce | flops 4864 | bytes 38912 | tf_op jit(solution)/shard_map/pmax | solution.py:26
  213.5 10.9 %exponential_reduce_fusion.2 = f32[4864]{0:T(1024)S(1)} fusion(f32[1024,4864]{1,0:T(8,128)} %get-tuple-element.10, f32[4864]{0:T(1024)S(1)} %pmax.29, f32[1024]{0:T(1024)S(1)} %add_subtract_fusion.1), kind=kLoop, calls=%fused_computation.3 | loop fusion | flops 14937344 | bytes 19965952 | tf_op jit(solution)/shard_map/reduce_sum | solution.py:27
  224.4 23.8 %psum.45 = f32[4864]{0:T(1024)S(1)} all-reduce(f32[4864]{0:T(1024)S(1)} %exponential_reduce_fusion.2), channel_id=1, replica_groups=mesh['src'=8,'tgt'=32] {'src'}, use_global_device_ids=true, to_apply=%region_11.0 | all-reduce | flops 4864 | bytes 38912 | tf_op jit(solution)/shard_map/psum | solution.py:27
  248.8 0.0 copy-done.1
  248.8 0.0 copy-done.2
  248.9 8.1 %add_reduce_fusion.1 = f32[1024]{0:T(1024)S(1)} fusion(f32[1024,4864]{1,0:T(8,128)} %get-tuple-element.10, f32[4864]{0:T(1024)S(1)} %select_subtract_fusion.1), kind=kLoop, calls=%fused_computation.6 | loop fusion | flops 9960448 | bytes 19946496 | tf_op jit(solution)/shard_map/reduce_max | solution.py:18
  257.0 69.7 %pmax.30 = f32[1024]{0:T(1024)S(1)} all-reduce(f32[1024]{0:T(1024)S(1)} %add_reduce_fusion.1), channel_id=1, replica_groups=mesh['src'=8,'tgt'=32] {'tgt'}, use_global_device_ids=true, to_apply=%region_13.0 | all-reduce | flops 1024 | bytes 8192 | tf_op jit(solution)/shard_map/pmax | solution.py:19
  326.6 10.0 %exponential_reduce_fusion.1 = f32[1024]{0:T(1024)S(1)} fusion(f32[1024,4864]{1,0:T(8,128)} %get-tuple-element.10, f32[1024]{0:T(1024)S(1)} %pmax.30, f32[4864]{0:T(1024)S(1)} %select_subtract_fusion.1), kind=kLoop, calls=%fused_computation.2 | loop fusion | flops 14941184 | bytes 19950592 | tf_op jit(solution)/shard_map/reduce_sum | solution.py:20
  336.6 71.6 %psum.46 = f32[1024]{0:T(1024)S(1)} all-reduce(f32[1024]{0:T(1024)S(1)} %exponential_reduce_fusion.1), channel_id=1, replica_groups=mesh['src'=8,'tgt'=32] {'tgt'}, use_global_device_ids=true, to_apply=%region_15.0 | all-reduce | flops 1024 | bytes 8192 | tf_op jit(solution)/shard_map/psum | solution.py:20
  408.3 8.3 %add_reduce_fusion = f32[4864]{0:T(1024)S(1)} fusion(f32[1024,4864]{1,0:T(8,128)} %get-tuple-element.10, f32[1024]{0:T(1024)S(1)} %get-tuple-element.8), kind=kLoop, calls=%fused_computation.5 | loop fusion | flops 9956608 | bytes 19946496 | tf_op jit(solution)/shard_map/reduce_max | solution.py:25
  416.6 23.6 %pmax.31 = f32[4864]{0:T(1024)S(1)} all-reduce(f32[4864]{0:T(1024)S(1)} %add_reduce_fusion), channel_id=1, replica_groups=mesh['src'=8,'tgt'=32] {'src'}, use_global_device_ids=true, to_apply=%region_17.0 | all-reduce | flops 4864 | bytes 38912 | tf_op jit(solution)/shard_map/pmax | solution.py:26
  440.2 10.9 %exponential_reduce_fusion = f32[4864]{0:T(1024)S(1)} fusion(f32[1024,4864]{1,0:T(8,128)} %get-tuple-element.10, f32[4864]{0:T(1024)S(1)} %pmax.31, f32[1024]{0:T(1024)S(1)} %get-tuple-element.8), kind=kLoop, calls=%fused_computation.1 | loop fusion | flops 14937344 | bytes 19965952 | tf_op jit(solution)/shard_map/reduce_sum | solution.py:27
  451.0 23.8 %psum.47 = f32[4864]{0:T(1024)S(1)} all-reduce(f32[4864]{0:T(1024)S(1)} %exponential_reduce_fusion), channel_id=1, replica_groups=mesh['src'=8,'tgt'=32] {'src'}, use_global_device_ids=true, to_apply=%region_19.0 | all-reduce | flops 4864 | bytes 38912 | tf_op jit(solution)/shard_map/psum | solution.py:27
  474.9 9.1 %fusion = f32[1024,256]{1,0:T(8,128)S(1)} fusion(bf16[4864,256]{1,0:T(8,128)(2,1)} %param.8, f32[1024,4864]{1,0:T(8,128)} %get-tuple-element.10, f32[4864]{0:T(1024)S(1)} %select_subtract_fusion, f32[1024]{0:T(1024)S(1)} %get-tuple-element.7), kind=kOutput, calls=%fused_computation.9 | convolution fusion | flops 2565079040 | bytes 23485440 | tf_op jit(solution)/shard_map/dot_general | solution.py:51
  484.0 0.1 collective-permute-start
  484.1 24.3 %collective-permute-done = f32[1024,256]{1,0:T(8,128)S(1)} collective-permute-done((f32[1024,256]{1,0:T(8,128)S(1)}, f32[1024,256]{1,0:T(8,128)S(1)}, u32[]{:S(2)}, u32[]{:S(2)}) %collective-permute-start) | collective-permute-done | bytes 1048608 | tf_op jit(solution)/shard_map/ppermute | solution.py:54
  508.4 0.1 add.112
  508.5 0.1 collective-permute-start.1
  508.6 23.0 %collective-permute-done.1 = f32[1024,256]{1,0:T(8,128)S(1)} collective-permute-done((f32[1024,256]{1,0:T(8,128)S(1)}, f32[1024,256]{1,0:T(8,128)S(1)}, u32[]{:S(2)}, u32[]{:S(2)}) %collective-permute-start.1) | collective-permute-done | bytes 1048608 | tf_op jit(solution)/shard_map/ppermute | solution.py:54
  531.6 0.1 add.113
  531.7 0.1 collective-permute-start.2
  531.8 20.9 %collective-permute-done.2 = f32[1024,256]{1,0:T(8,128)S(1)} collective-permute-done((f32[1024,256]{1,0:T(8,128)S(1)}, f32[1024,256]{1,0:T(8,128)S(1)}, u32[]{:S(2)}, u32[]{:S(2)}) %collective-permute-start.2) | collective-permute-done | bytes 1048608 | tf_op jit(solution)/shard_map/ppermute | solution.py:54
  552.7 0.1 add.114
  552.9 0.1 collective-permute-start.3
  553.0 83.6 %collective-permute-done.3 = f32[1024,256]{1,0:T(8,128)S(1)} collective-permute-done((f32[1024,256]{1,0:T(8,128)S(1)}, f32[1024,256]{1,0:T(8,128)S(1)}, u32[]{:S(2)}, u32[]{:S(2)}) %collective-permute-start.3) | collective-permute-done | bytes 1048608 | tf_op jit(solution)/shard_map/ppermute | solution.py:54
  636.5 0.1 add.115
  636.7 0.1 collective-permute-start.4
  636.8 38.4 %collective-permute-done.4 = f32[1024,256]{1,0:T(8,128)} collective-permute-done((f32[1024,256]{1,0:T(8,128)S(1)}, f32[1024,256]{1,0:T(8,128)}, u32[]{:S(2)}, u32[]{:S(2)}) %collective-permute-start.4) | collective-permute-done | bytes 1048608 | tf_op jit(solution)/shard_map/ppermute | solution.py:54
  675.2 1.4 dynamic-slice_add_fusion
  (4 shorter events, 0.1 us)
Async XLA Ops:
  0.0 2.8 copy-start
  2.8 179.4 %copy-start.3 = (s32[1024]{0:T(1024)S(1)}, s32[1024]{0:T(1024)}, u32[]{:S(2)}) copy-start(s32[1024]{0:T(1024)} %param.10) | copy-start | bytes 12292
  182.2 66.6 %copy-start.1 = (s32[4864]{0:T(1024)S(1)}, s32[4864]{0:T(1024)}, u32[]{:S(2)}) copy-start(s32[4864]{0:T(1024)} %param.11) | copy-start | bytes 58372
  182.2 66.6 %copy-start.2 = (f32[4864]{0:T(1024)S(1)}, f32[4864]{0:T(1024)}, u32[]{:S(2)}) copy-start(f32[4864]{0:T(1024)} %param.9) | copy-start | bytes 58372
  484.0 24.4 %collective-permute-start = (f32[1024,256]{1,0:T(8,128)S(1)}, f32[1024,256]{1,0:T(8,128)S(1)}, u32[]{:S(2)}, u32[]{:S(2)}) collective-permute-start(f32[1024,256]{1,0:T(8,128)S(1)} %fusion), channel_id=1, source_target_pairs={{0,1},{1,0},{2,3},{3,2},{4,5},{5,4},{6,7},{7,6},{8,9},{9,8},{10,11... | collective-permute-start | bytes 3145736 | tf_op jit(solution)/shard_map/ppermute | solution.py:54
  508.5 23.1 %collective-permute-start.1 = (f32[1024,256]{1,0:T(8,128)S(1)}, f32[1024,256]{1,0:T(8,128)S(1)}, u32[]{:S(2)}, u32[]{:S(2)}) collective-permute-start(f32[1024,256]{1,0:T(8,128)S(1)} %add.112), channel_id=1, source_target_pairs={{0,2},{1,3},{2,0},{3,1},{4,6},{5,7},{6,4},{7,5},{8,10},{9,11},{10,... | collective-permute-start | bytes 3145736 | tf_op jit(solution)/shard_map/ppermute | solution.py:54
  531.7 21.0 %collective-permute-start.2 = (f32[1024,256]{1,0:T(8,128)S(1)}, f32[1024,256]{1,0:T(8,128)S(1)}, u32[]{:S(2)}, u32[]{:S(2)}) collective-permute-start(f32[1024,256]{1,0:T(8,128)S(1)} %add.113), channel_id=1, source_target_pairs={{0,4},{1,5},{2,6},{3,7},{4,0},{5,1},{6,2},{7,3},{8,12},{9,13},{10,... | collective-permute-start | bytes 3145736 | tf_op jit(solution)/shard_map/ppermute | solution.py:54
  552.9 83.7 %collective-permute-start.3 = (f32[1024,256]{1,0:T(8,128)S(1)}, f32[1024,256]{1,0:T(8,128)S(1)}, u32[]{:S(2)}, u32[]{:S(2)}) collective-permute-start(f32[1024,256]{1,0:T(8,128)S(1)} %add.114), channel_id=1, source_target_pairs={{0,8},{1,9},{2,10},{3,11},{4,12},{5,13},{6,14},{7,15},{8,0},{9,1},... | collective-permute-start | bytes 3145736 | tf_op jit(solution)/shard_map/ppermute | solution.py:54
  636.7 38.5 %collective-permute-start.4 = (f32[1024,256]{1,0:T(8,128)S(1)}, f32[1024,256]{1,0:T(8,128)}, u32[]{:S(2)}, u32[]{:S(2)}) collective-permute-start(f32[1024,256]{1,0:T(8,128)S(1)} %add.115), channel_id=1, source_target_pairs={{0,16},{1,17},{2,18},{3,19},{4,20},{5,21},{6,22},{7,23},{8,24},{9,... | collective-permute-start | bytes 3145736 | tf_op jit(solution)/shard_map/ppermute | solution.py:54
